TPU v7x, 32 devices: a whole 2x2x4 slice. The times are simulated.
32 devices in a mesh: depth: 4 (over z), wide: 8 (over y, x, core).
Axes of the slice: x: 2, y: 2, z: 4, core: 2. Of those that a mesh axis runs over, the one named last changes fastest.
Arguments:
- density: float32 [4, 4096, 4096], P('depth', 'wide'), may hold values from -4 to 4
- layer_top: float32 [4], P('depth'), may hold values from 0.75 to 1.5
- layer_thick: float32 [4], P('depth'), may hold values from 1.5 to 3
- sample_row: int32 [32, 256], P(('depth', 'wide')), may hold values from 0 to 127
- sample_col: int32 [32, 256], P(('depth', 'wide')), may hold values from 0 to 4095
- sample_frac: int32 [32, 2, 256], P(('depth', 'wide')), may hold values from 0 to 15
- sample_owner: int32 [32, 256, 1], P(('depth', 'wide')), may hold values from 0 to 7; in each aligned block of 256 rows (0 to 255, 256 to 511, ..., all dimensions but the last counted through in order) at most 64 rows name the same one
Outputs:
- gradient_grid: float32 [6, 4096, 4096], P(None, ('depth', 'wide'))
- line_samples: float32 [6, 32, 512], P(None, ('depth', 'wide'))
Inputs may be any that keep to these rules, and one draw needn't show every extreme that they name: `sample_owner`: among the 256 samples of one tile no owner is named more than 64 times, a bound that some block reaches.
All inputs are finite; a program needn't handle non-finite values.
Results may differ from a plain program's by a relative error of at most 0.0001.
Values sent between devices are 32-bit elements; how exact they have to be, the bound alone decides.
No kernel may reach another device: no remote copies, remote signals or barrier semaphores. Data moves between devices by JAX's collectives and lax.ppermute only.
A program may use at most 320 MiB of HBM per device.

v0:
```python
import math
import jax
import jax.numpy as jnp
from jax import lax
from jax.sharding import PartitionSpec as P

RADIX = 128
QLEV = 16
HIGH = lax.Precision.HIGHEST


def padded_2(block, sides, width):
    for axis, dim in sides:
        count = lax.axis_size(axis)
        forward = [(i, i + 1) for i in range(count - 1)]
        forward.append((count - 1, 0))
        backward = [(target, source) for source, target in forward]
        low = lax.ppermute(
            lax.slice_in_dim(block, block.shape[dim] - width, None, axis=dim), axis, forward
        )
        high = lax.ppermute(lax.slice_in_dim(block, 0, width, axis=dim), axis, backward)
        block = jnp.concatenate([low, block, high], axis=dim)
    return block


def product(formula, operand_a, operand_b):
    return jnp.einsum(formula, operand_a, operand_b, precision=HIGH)


def complex_product(formula, complex_pair, table_pair):
    real_part = product(formula, complex_pair[0], table_pair[0]) - product(
        formula, complex_pair[1], table_pair[1]
    )
    imag_part = product(formula, complex_pair[0], table_pair[1]) + product(
        formula, complex_pair[1], table_pair[0]
    )
    return (real_part, imag_part)


def phase_table(row_count, col_count, period, orient):
    left_ids = jnp.arange(row_count, dtype=jnp.int32)[:, None]
    right_ids = jnp.arange(col_count, dtype=jnp.int32)[None, :]
    angles = (left_ids * right_ids % period).astype(jnp.float32) * (2.0 * math.pi / period)
    return (jnp.cos(angles), orient * jnp.sin(angles))


def times_table(complex_pair, table_pair):
    return (
        complex_pair[0] * table_pair[0] - complex_pair[1] * table_pair[1],
        complex_pair[0] * table_pair[1] + complex_pair[1] * table_pair[0],
    )


def column_forward(complex_pair):
    grid_len = complex_pair[0].shape[0]
    outer_len = grid_len // RADIX
    item_count = complex_pair[0].shape[2]
    columns = (
        complex_pair[0].reshape(outer_len, RADIX, item_count),
        complex_pair[1].reshape(outer_len, RADIX, item_count),
    )
    partial_value = complex_product(
        "bcd,ab->acd", columns, phase_table(outer_len, outer_len, outer_len, -1.0)
    )
    twiddles = phase_table(outer_len, RADIX, grid_len, -1.0)
    partial_value = times_table(partial_value, (twiddles[0][:, :, None], twiddles[1][:, :, None]))
    return complex_product("abd,bc->acd", partial_value, phase_table(RADIX, RADIX, RADIX, -1.0))


def row_inverse(complex_pair):
    dims_in = complex_pair[0].shape
    grid_len = dims_in[-1]
    outer_len = grid_len // RADIX
    flat_dims = (-1, outer_len, RADIX)
    row_values = (complex_pair[0].reshape(flat_dims), complex_pair[1].reshape(flat_dims))
    partial_value = complex_product(
        "zab,cb->zac", row_values, phase_table(RADIX, RADIX, RADIX, 1.0)
    )
    partial_value = times_table(partial_value, phase_table(outer_len, RADIX, grid_len, 1.0))
    partial_value = complex_product(
        "zbc,ab->zac", partial_value, phase_table(outer_len, outer_len, outer_len, 1.0)
    )
    return (partial_value[0].reshape(dims_in), partial_value[1].reshape(dims_in))


def column_inverse_start(complex_pair):
    outer_len = complex_pair[0].shape[1]
    partial_value = complex_product(
        "jabd,cb->jacd", complex_pair, phase_table(RADIX, RADIX, RADIX, 1.0)
    )
    twiddles = phase_table(outer_len, RADIX, outer_len * RADIX, 1.0)
    return times_table(partial_value, (twiddles[0][:, :, None], twiddles[1][:, :, None]))


def wavenumber(wave_index, grid_len):
    signed_ids = jnp.where(wave_index < grid_len // 2, wave_index, wave_index - grid_len).astype(
        jnp.float32
    )
    full_wave = signed_ids * (2.0 * math.pi / grid_len)
    odd_wave = jnp.where(wave_index == grid_len // 2, 0.0, full_wave)
    return (full_wave, odd_wave)


def channel_spectra(continued, full_x, full_y, odd_x, odd_y, safe_square, safe_root):
    real_part, imag_part = continued
    coef_xx = -full_x * full_x / safe_square
    coef_yy = -full_y * full_y / safe_square
    coef_xy = -odd_x * odd_y / safe_square
    slope_x = odd_x / safe_root
    slope_y = odd_y / safe_root
    first_pair = (
        real_part * coef_xx - imag_part * coef_yy,
        real_part * coef_yy + imag_part * coef_xx,
    )
    second_pair = (real_part * coef_xy - imag_part, real_part + imag_part * coef_xy)
    third_pair = (
        -real_part * slope_y - imag_part * slope_x,
        real_part * slope_x - imag_part * slope_y,
    )
    return (
        jnp.stack([first_pair[0], second_pair[0], third_pair[0]]),
        jnp.stack([first_pair[1], second_pair[1], third_pair[1]]),
    )


def ordered_channels(real_fields, imag_fields):
    return jnp.concatenate(
        [real_fields, imag_fields[0:1], imag_fields[2:3], imag_fields[1:2]], axis=0
    )


def cubic_kernel(distance):
    near_part = (1.5 * distance - 2.5) * distance * distance + 1.0
    far_part = ((-0.5 * distance + 2.5) * distance - 4.0) * distance + 2.0
    return jnp.where(distance <= 1.0, near_part, jnp.where(distance < 2.0, far_part, 0.0))


def weight_rows(levels):
    level_ids = jnp.arange(levels, dtype=jnp.int32)
    offsets = (level_ids.astype(jnp.float32) + 0.5) / levels - 0.5
    bases = jnp.where(level_ids < levels // 2, -1.0, 0.0).astype(jnp.float32)
    fraction = offsets - bases
    tap_pos = jnp.arange(4, dtype=jnp.int32).astype(jnp.float32) - 1.0
    return cubic_kernel(jnp.abs(fraction[:, None] - tap_pos[None, :]))


def per_device(density, layer_top, layer_thick, sample_row, sample_col, sample_frac, sample_owner):
    wide_count = lax.axis_size("wide")
    depth_count = lax.axis_size("depth")
    rows_here = density.shape[1]
    grid_len = density.shape[2]
    outer_len = grid_len // RADIX
    local_cols = grid_len // wide_count
    tile_rows = rows_here // depth_count
    layer_field = density[0].reshape(rows_here, outer_len, RADIX)
    first_table = phase_table(outer_len, outer_len, outer_len, -1.0)
    partial_value = (
        product("rbc,ab->rac", layer_field, first_table[0]),
        product("rbc,ab->rac", layer_field, first_table[1]),
    )
    partial_value = times_table(partial_value, phase_table(outer_len, RADIX, grid_len, -1.0))
    partial_value = complex_product(
        "rab,bc->rac", partial_value, phase_table(RADIX, RADIX, RADIX, -1.0)
    )
    row_spectra = (
        partial_value[0].reshape(rows_here, wide_count, local_cols),
        partial_value[1].reshape(rows_here, wide_count, local_cols),
    )
    spectrum = column_forward(
        (
            lax.all_to_all(row_spectra[0], "wide", split_axis=1, concat_axis=0, tiled=True),
            lax.all_to_all(row_spectra[1], "wide", split_axis=1, concat_axis=0, tiled=True),
        )
    )
    position = lax.axis_index("wide") * local_cols + jnp.arange(local_cols, dtype=jnp.int32)
    index_x = position // RADIX + outer_len * (position % RADIX)
    index_y = (
        jnp.arange(outer_len, dtype=jnp.int32)[:, None]
        + outer_len * jnp.arange(RADIX, dtype=jnp.int32)[None, :]
    )
    full_x, odd_x = wavenumber(index_x, grid_len)
    full_y, odd_y = wavenumber(index_y, grid_len)
    full_x = full_x[None, None, :]
    odd_x = odd_x[None, None, :]
    full_y = full_y[:, :, None]
    odd_y = odd_y[:, :, None]
    squared = full_x * full_x + full_y * full_y
    magnitude = jnp.sqrt(squared)
    safe_square = jnp.where(squared > 0.0, squared, 1.0)
    safe_root = jnp.sqrt(safe_square)
    continuation = (
        2.0
        * math.pi
        / (grid_len * grid_len)
        * (1.0 - jnp.exp(-magnitude * layer_thick[0]))
        * jnp.exp(-magnitude * layer_top[0])
    )
    continued = (spectrum[0] * continuation, spectrum[1] * continuation)
    summed = lax.psum((continued[0], continued[1]), "depth")
    channels = channel_spectra(summed, full_x, full_y, odd_x, odd_y, safe_square, safe_root)
    partial_value = column_inverse_start(channels)
    row_share = outer_len // depth_count
    row_start = lax.axis_index("depth") * row_share
    back_table = phase_table(outer_len, outer_len, outer_len, 1.0)
    share_table = (
        lax.dynamic_slice_in_dim(back_table[0], row_start, row_share, 0),
        lax.dynamic_slice_in_dim(back_table[1], row_start, row_share, 0),
    )
    partial_value = complex_product("jbcd,ab->jacd", partial_value, share_table)
    row_blocks = (
        partial_value[0].reshape(3, wide_count, tile_rows, local_cols),
        partial_value[1].reshape(3, wide_count, tile_rows, local_cols),
    )
    row_fields = row_inverse(
        (
            lax.all_to_all(row_blocks[0], "wide", split_axis=1, concat_axis=3, tiled=True),
            lax.all_to_all(row_blocks[1], "wide", split_axis=1, concat_axis=3, tiled=True),
        )
    )
    gradient = ordered_channels(row_fields[0], row_fields[1]).reshape(6, tile_rows, grid_len)
    padded = padded_2(gradient, ((("depth", "wide"), 1),), 2)
    weight_table = weight_rows(QLEV)
    level_ids = jnp.arange(QLEV, dtype=jnp.int32)[None, :]
    frac_y = sample_frac[0, 0]
    frac_x = sample_frac[0, 1]
    weight_y = jnp.dot(
        (frac_y[:, None] == level_ids).astype(jnp.float32), weight_table, precision=HIGH
    )
    weight_x = jnp.dot(
        (frac_x[:, None] == level_ids).astype(jnp.float32), weight_table, precision=HIGH
    )
    base_y = jnp.where(frac_y < QLEV // 2, -1, 0).astype(jnp.int32)
    base_x = jnp.where(frac_x < QLEV // 2, -1, 0).astype(jnp.int32)
    tap_ids = jnp.arange(4, dtype=jnp.int32)[None, :]
    row_ids = (sample_row[0] + base_y + 1)[:, None] + tap_ids
    col_ids = ((sample_col[0] + base_x - 1)[:, None] + tap_ids) % grid_len
    neighbours = padded[:, row_ids[:, :, None], col_ids[:, None, :]]
    interpolated = jnp.einsum("csab,sa,sb->cs", neighbours, weight_y, weight_x, precision=HIGH)
    sample_count = sample_row.shape[1]
    capacity = max(2 * sample_count // wide_count, 2)
    slot_total = wide_count * capacity
    owner_ids = sample_owner[0, :, 0]
    owner_marks = (owner_ids[:, None] == jnp.arange(wide_count, dtype=jnp.int32)[None, :]).astype(
        jnp.int32
    )
    earlier = jnp.cumsum(owner_marks, axis=0) - owner_marks
    slot_ids = jnp.sum(earlier * owner_marks, axis=1)
    target = owner_ids * capacity + slot_ids
    placement = (target[:, None] == jnp.arange(slot_total, dtype=jnp.int32)[None, :]).astype(
        jnp.float32
    )
    outgoing = jnp.dot(interpolated, placement, precision=HIGH).reshape(6, wide_count, capacity)
    arrived = lax.all_to_all(outgoing, "wide", split_axis=1, concat_axis=1, tiled=True)
    return (gradient, arrived.reshape(6, 1, slot_total))


def solution(mesh):
    in_specs = (
        P("depth", "wide", None),
        P("depth"),
        P("depth"),
        P(("depth", "wide"), None),
        P(("depth", "wide"), None),
        P(("depth", "wide"), None, None),
        P(("depth", "wide"), None, None),
    )
    out_specs = (P(None, ("depth", "wide"), None), P(None, ("depth", "wide"), None))
    return jax.shard_map(
        per_device, mesh=mesh, in_specs=in_specs, out_specs=out_specs, check_vma=False
    )
```

profile of v0, /device:TPU:0, one launch (start us, length us, event | category | flops | bytes accessed | tf_op | source)
XLA Modules:
  0.0 1574.2 jit_solution(17820646528729374179)
XLA Ops:
  79.8 18.6 %fusion.46 = f32[512,32,128]{0,2,1:T(8,128)S(1)} fusion(f32[512,32,128]{2,1,0:T(8,128)} %copy-done.5), kind=kOutput, calls=%fused_computation.69 | convolution fusion | flops 3221471232 | bytes 16777216 | tf_op jit(solution)/shard_map/rab,bc->rac/dot_general | solution.py:27
  98.5 21.9 %fusion.68 = f32[512,32,128]{0,2,1:T(8,128)} fusion(f32[512,32,128]{0,2,1:T(8,128)S(1)} %fusion.46, f32[512,32,128]{2,1,0:T(8,128)} %copy-done.2), kind=kOutput, calls=%fused_computation.97 | convolution fusion | flops 3223552000 | bytes 25165824 | tf_op jit(solution)/shard_map/rab,bc->rac/dot_general | solution.py:27
  129.4 44.9 %all-to-all-done.1 = f32[512,8,512]{2,0,1:T(8,128)} async-done(((f32[512,8,512]{2,0,1:T(8,128)}), f32[512,8,512]{2,0,1:T(8,128)}, u32[]{:S(2)}, u32[]{:S(2)}) %all-to-all-start.1) | async-done | bytes 8388640 | tf_op jit(solution)/shard_map/all_to_all | solution.py:172
  180.9 17.1 %fusion.36 = f32[32,128,512]{2,0,1:T(8,128)} fusion(f32[32,128,512]{2,1,0:T(8,128)} %bitcast.22), kind=kOutput, calls=%fused_computation.59 | convolution fusion | flops 805320704 | bytes 16777216 | tf_op jit(solution)/shard_map/bcd,ab->acd/dot_general | solution.py:27
  198.0 17.6 %fusion.38 = f32[32,128,512]{2,0,1:T(8,128)} fusion(f32[32,128,512]{2,1,0:T(8,128)} %bitcast.22), kind=kOutput, calls=%fused_computation.61 | convolution fusion | flops 805321728 | bytes 16777216 | tf_op jit(solution)/shard_map/bcd,ab->acd/dot_general | solution.py:27
  215.7 57.7 %all-to-all-done = f32[512,8,512]{2,0,1:T(8,128)} async-done(((f32[512,8,512]{2,0,1:T(8,128)}), f32[512,8,512]{2,0,1:T(8,128)}, u32[]{:S(2)}, u32[]{:S(2)}) %all-to-all-start) | async-done | bytes 8388640 | tf_op jit(solution)/shard_map/all_to_all | solution.py:171
  273.4 17.5 %fusion.42 = f32[32,128,512]{2,0,1:T(8,128)} fusion(f32[32,128,512]{2,1,0:T(8,128)} %bitcast.16), kind=kOutput, calls=%fused_computation.65 | convolution fusion | flops 805320704 | bytes 16777216 | tf_op jit(solution)/shard_map/bcd,ab->acd/dot_general | solution.py:27
  290.9 24.4 %multiply_subtract_fusion = (f32[32,128,512]{2,0,1:T(8,128)}, f32[32,128,512]{2,0,1:T(8,128)}) fusion(f32[32,128]{0,1:T(8,128)S(1)} %copy.142, f32[32,128]{0,1:T(8,128)S(1)} %copy.139, f32[32,128,512]{2,0,1:T(8,128)} %fusion.36, f32[32,128,512]{2,0,1:T(8,128)} %fusion.42, f32[32,128,512]{2,0,1:T(8,128)} %fusion.38, f32[32,128,512]{2,1,0:T(8,128)} %bitcast.16), kind=kOutput, calls=%fused_computation.48 | convolution fusion | flops 822098944 | bytes 50364416 | tf_op jit(solution)/shard_map/bcd,ab->acd/dot_general | solution.py:27
  315.3 18.1 %fusion.28 = f32[128,32,512]{2,0,1:T(8,128)S(1)} fusion(f32[32,128,512]{2,0,1:T(8,128)} %get-tuple-element.15), kind=kOutput, calls=%fused_computation.51 | convolution fusion | flops 3221454848 | bytes 16777216 | tf_op jit(solution)/shard_map/abd,bc->acd/dot_general | solution.py:27
  345.8 18.2 %bitcast_multiply_fusion.5 = f32[32,128,512]{2,1,0:T(8,128)} fusion(f32[128,32,512]{2,0,1:T(8,128)S(1)} %fusion.30, f32[]{:T(128)} %bitcast.208, f32[]{:T(128)} %bitcast.210, f32[32,128]{1,0:T(8,128)S(1)} %get-tuple-element.40, f32[512]{0:T(512)S(1)} %fusion.224, f32[32,128,512]{2,0,1:T(8,128)S(1)} %bitcast.220), kind=kOutput, calls=%fused_computation.40 | convolution fusion | flops 3240329216 | bytes 25184264 | tf_op jit(solution)/shard_map/abd,bc->acd/dot_general | solution.py:27
  364.0 18.5 %bitcast_multiply_fusion.4 = f32[32,128,512]{2,1,0:T(8,128)} fusion(f32[128,32,512]{2,0,1:T(8,128)S(1)} %fusion.28, f32[]{:T(128)} %bitcast.209, f32[]{:T(128)} %bitcast.211, f32[32,128]{1,0:T(8,128)S(1)} %get-tuple-element.40, f32[512]{0:T(512)S(1)} %fusion.224, f32[32,128,512]{2,0,1:T(8,128)S(1)} %bitcast.220), kind=kOutput, calls=%fused_computation.39 | convolution fusion | flops 3240345600 | bytes 25184264 | tf_op jit(solution)/shard_map/abd,bc->acd/dot_general | solution.py:27
  382.8 563.3 %all-reduce.3.cloned.1.call-done = (f32[32,128,512]{2,1,0:T(8,128)}, f32[32,128,512]{2,1,0:T(8,128)}) async-done(((f32[32,128,512]{2,1,0:T(8,128)}, f32[32,128,512]{2,1,0:T(8,128)}), (f32[32,128,512]{2,1,0:T(8,128)}, f32[32,128,512]{2,1,0:T(8,128)})) %all-reduce.3.cloned.1.call-update) | async-done | bytes 16777232 | tf_op jit(solution)/shard_map/psum | solution.py:199
  946.1 21.0 %add_bitcast_fusion.1 = (f32[1,32,128,512]{3,2,1,0:T(8,128)}, f32[1,32,128,512]{3,2,1,0:T(8,128)S(1)}, f32[1,32,128,512]{3,2,1,0:T(8,128)}, f32[1,32,128,512]{3,...) fusion(f32[32,128,512]{2,1,0:T(8,128)} %get-tuple-element.10, ...), kind=kLoop, calls=%fused_computation.43 | loop fusion | flops 54525952 | bytes 67166208 | tf_op jit(solution)/shard_map/stack | solution.py:122
  967.1 34.1 %fusion.10 = f32[128,3,32,512]{3,0,2,1:T(8,128)} fusion(f32[1,32,128,512]{3,2,1,0:T(8,128)} %get-tuple-element.28, f32[1,32,128,512]{3,2,1,0:T(8,128)} %get-tuple-element.31, f32[1,32,128,512]{3,2,1,0:T(8,128)} %get-tuple-element.18), kind=kOutput, calls=%fused_computation.18 | convolution fusion | flops 9676488704 | bytes 50331648 | tf_op jit(solution)/shard_map/jabd,cb->jacd/dot_general | solution.py:27
  1001.2 29.1 %fusion.11 = f32[128,3,32,512]{3,0,2,1:T(8,128)} fusion(f32[1,32,128,512]{3,2,1,0:T(8,128)} %get-tuple-element.28, f32[1,32,128,512]{3,2,1,0:T(8,128)} %get-tuple-element.31, f32[1,32,128,512]{3,2,1,0:T(8,128)} %get-tuple-element.18), kind=kOutput, calls=%fused_computation.19 | convolution fusion | flops 9676488704 | bytes 50331648 | tf_op jit(solution)/shard_map/jabd,cb->jacd/dot_general | solution.py:27
  1030.4 28.4 %fusion.13 = f32[128,3,32,512]{3,0,2,1:T(8,128)} fusion(f32[1,32,128,512]{3,2,1,0:T(8,128)S(1)} %get-tuple-element.29, f32[1,32,128,512]{3,2,1,0:T(8,128)} %get-tuple-element.30, f32[1,32,128,512]{3,2,1,0:T(8,128)S(1)} %get-tuple-element.19), kind=kOutput, calls=%fused_computation.21 | convolution fusion | flops 9676488704 | bytes 50331648 | tf_op jit(solution)/shard_map/jabd,cb->jacd/dot_general | solution.py:27
  1058.8 60.9 %fusion = (f32[3,32,128,512]{3,2,1,0:T(8,128)}, f32[3,32,128,512]{3,2,1,0:T(8,128)}) fusion(f32[32,128]{1,0:T(8,128)S(1)} %fusion.189, f32[32,128]{1,0:T(8,128)S(1)} %get-tuple-element.43, f32[128,3,32,512]{3,0,2,1:T(8,128)} %fusion.10, f32[128,3,32,512]{3,0,2,1:T(8,128)} %fusion.13, f32[128,3,32,512]{3,0,2,1:T(8,128)} %fusion.11, ...), kind=kOutput, calls=%fused_computation.5 | convolution fusion | flops 9726820352 | bytes 151027712 | tf_op jit(solution)/shard_map/jabd,cb->jacd/dot_general | solution.py:27
  1119.6 34.6 %fusion.2 = f32[8,3,128,512]{3,0,2,1:T(8,128)} fusion(f32[3,32,128,512]{3,2,1,0:T(8,128)} %get-tuple-element.13, f32[32,32]{1,0:T(8,128)S(1)} %fusion.192, s32[]{:T(128)S(6)} %select_n.307), kind=kOutput, calls=%fused_computation.10 | convolution fusion | flops 603979776 | bytes 31461380 | tf_op jit(solution)/shard_map/jbcd,ab->jacd/dot_general | solution.py:27
  1154.2 26.1 %add_bitcast_fusion.4 = f32[3,8,128,512]{3,1,2,0:T(8,128)S(1)} fusion(f32[8,3,128,512]{3,0,2,1:T(8,128)} %fusion.2, f32[3,32,128,512]{3,2,1,0:T(8,128)S(1)} %copy-done, f32[32,32]{1,0:T(8,128)S(1)} %fusion.191, s32[]{:T(128)S(6)} %select_n.307), kind=kOutput, calls=%fused_computation.79 | convolution fusion | flops 605552640 | bytes 37752836 | tf_op jit(solution)/shard_map/jbcd,ab->jacd/dot_general | solution.py:27
  1191.5 33.3 %fusion.4 = f32[8,3,128,512]{3,0,2,1:T(8,128)S(1)} fusion(f32[3,32,128,512]{3,2,1,0:T(8,128)} %get-tuple-element.13, f32[32,32]{1,0:T(8,128)S(1)} %fusion.191, s32[]{:T(128)S(6)} %select_n.307), kind=kOutput, calls=%fused_computation.12 | convolution fusion | flops 603979776 | bytes 31461380 | tf_op jit(solution)/shard_map/jbcd,ab->jacd/dot_general | solution.py:27
  1224.8 33.7 %subtract_bitcast_fusion.6 = f32[3,8,128,512]{3,1,2,0:T(8,128)S(1)} fusion(f32[8,3,128,512]{3,0,2,1:T(8,128)S(1)} %fusion.4, f32[3,32,128,512]{3,2,1,0:T(8,128)} %get-tuple-element.12, f32[32,32]{1,0:T(8,128)S(1)} %fusion.192, s32[]{:T(128)S(6)} %select_n.307), kind=kOutput, calls=%fused_computation.80 | convolution fusion | flops 605552640 | bytes 37752836 | tf_op jit(solution)/shard_map/jbcd,ab->jacd/dot_general | solution.py:27
  1317.4 24.1 %all-to-all-done.2 = f32[3,8,128,512]{3,2,0,1:T(8,128)} async-done(((f32[3,8,128,512]{3,2,0,1:T(8,128)}), f32[3,8,128,512]{3,2,0,1:T(8,128)}, u32[]{:S(2)}, u32[]{:S(2)}) %all-to-all-start.2) | async-done | bytes 6291488 | tf_op jit(solution)/shard_map/all_to_all | solution.py:216
  1478.7 55.1 %gather_fusion = f32[4096,6]{0,1:T(8,128)S(1)} fusion(f32[6,132,4096]{2,0,1:T(8,128)} %pad_maximum_fusion.6, s32[4096]{0:T(1024)S(1)} %reshape.412), kind=kCustom, calls=%fused_computation | custom fusion | bytes 229376 | tf_op jit(solution)/shard_map/gather | solution.py:237
  1547.1 17.8 %copy.175 = f32[6,128,4096]{2,1,0:T(8,128)} copy(f32[6,128,4096]{2,0,1:T(8,128)} %copy-done.1) | data formatting | bytes 25165824
  (122 shorter events, 321.8 us)
Async XLA Ops:
  12.5 9.6 copy-start.6
  35.2 14.0 copy-start.5
  35.2 14.0 copy-start.2
  74.7 99.7 %all-to-all-start.1 = ((f32[512,8,512]{2,0,1:T(8,128)}), f32[512,8,512]{2,0,1:T(8,128)}, u32[]{:S(2)}, u32[]{:S(2)}) async-start(f32[512,8,512]{2,0,1:T(8,128)} %copy.137), calls=%async_computation.1 | async-start | bytes 16777216 | tf_op jit(solution)/shard_map/all_to_all | solution.py:172
  174.4 99.0 %all-to-all-start = ((f32[512,8,512]{2,0,1:T(8,128)}), f32[512,8,512]{2,0,1:T(8,128)}, u32[]{:S(2)}, u32[]{:S(2)}) async-start(f32[512,8,512]{2,0,1:T(8,128)} %copy.131), calls=%async_computation | async-start | bytes 16777216 | tf_op jit(solution)/shard_map/all_to_all | solution.py:171
  179.3 766.8 %all-reduce.3.cloned.1.call-start = ((), (), s32[]{:S(2)}) async-start(), calls=%async_computation.5 | async-start | bytes 33554432 | tf_op jit(solution)/shard_map/psum | solution.py:199
  315.3 18.1 %copy-start.7 = (f32[32,128,512]{2,0,1:T(8,128)S(1)}, f32[32,128,512]{2,0,1:T(8,128)}, u32[]{:S(2)}) copy-start(f32[32,128,512]{2,0,1:T(8,128)} %get-tuple-element.15) | copy-start | bytes 25165828
  315.3 30.5 %slice-start.2 = ((s8[8388608]{0:T(1024)(128)(4,1)}), s8[4194304]{0:T(1024)(128)(4,1)S(1)}, s32[]{:S(2)}) async-start(s8[8388608]{0:T(1024)(128)(4,1)} %bitcast.219), calls=%async_computation.8 | async-start | bytes 8388608
  333.4 12.4 slice-start.3
  967.1 63.2 %copy-start.3 = (f32[1,32,128,512]{3,2,1,0:T(8,128)}, f32[1,32,128,512]{3,2,1,0:T(8,128)S(1)}, u32[]{:S(2)}) copy-start(f32[1,32,128,512]{3,2,1,0:T(8,128)S(1)} %get-tuple-element.19) | copy-start | bytes 25165828
  967.1 63.2 %copy-start.4 = (f32[1,32,128,512]{3,2,1,0:T(8,128)}, f32[1,32,128,512]{3,2,1,0:T(8,128)S(1)}, u32[]{:S(2)}) copy-start(f32[1,32,128,512]{3,2,1,0:T(8,128)S(1)} %get-tuple-element.29) | copy-start | bytes 25165828
  1119.6 34.6 %copy-start = (f32[3,32,128,512]{3,2,1,0:T(8,128)S(1)}, f32[3,32,128,512]{3,2,1,0:T(8,128)}, u32[]{:S(2)}) copy-start(f32[3,32,128,512]{3,2,1,0:T(8,128)} %get-tuple-element.12) | copy-start | bytes 75497472
  1186.7 78.0 %all-to-all-start.3 = ((f32[3,8,128,512]{3,2,0,1:T(8,128)}), f32[3,8,128,512]{3,2,0,1:T(8,128)}, u32[]{:S(2)}, u32[]{:S(2)}) async-start(f32[3,8,128,512]{3,2,0,1:T(8,128)} %copy.158), calls=%async_computation.3 | async-start | bytes 12582912 | tf_op jit(solution)/shard_map/all_to_all | solution.py:217
  1264.7 6.0 copy-start.13
  1264.7 6.0 copy-start.14
  1264.8 76.7 %all-to-all-start.2 = ((f32[3,8,128,512]{3,2,0,1:T(8,128)}), f32[3,8,128,512]{3,2,0,1:T(8,128)}, u32[]{:S(2)}, u32[]{:S(2)}) async-start(f32[3,8,128,512]{3,2,0,1:T(8,128)} %copy.153), calls=%async_computation.2 | async-start | bytes 12582912 | tf_op jit(solution)/shard_map/all_to_all | solution.py:216
  1291.2 13.7 copy-start.8
  1357.4 13.9 copy-start.9
  1386.8 19.0 %slice-start = ((s8[6291456]{0:T(1024)(128)(4,1)}), s8[4194304]{0:T(1024)(128)(4,1)S(1)}, s32[]{:S(2)}) async-start(s8[6291456]{0:T(1024)(128)(4,1)} %bitcast.214), calls=%async_computation.6 | async-start | bytes 8388608
  1396.1 9.7 slice-start.1
  1462.6 9.6 copy-start.1
  1462.7 9.5 collective-permute-start
  1462.8 9.5 collective-permute-start.1
  1543.5 21.4 %all-to-all-start.4 = ((f32[8,1,384]{2,1,0:T(1,128)}), f32[8,1,384]{2,1,0:T(1,128)S(1)}, u32[]{:S(2)}, u32[]{:S(2)}) async-start(f32[8,1,384]{2,1,0:T(1,128)} %reshape.439), calls=%async_computation.4 | async-start | bytes 24576 | tf_op jit(solution)/shard_map/all_to_all | solution.py:253
  (3 other events, 17.0 us)
Sparse Core Ops, SparseCore 0:
  382.6 563.4 all-reduce.2
where the time goes:
time: 1580 us; the launch traced here: 1570 us
  waiting for transfers between devices  694 us (44%)
  matrix products  619 us (39%)
  local copies, waits for them, and re-layouts  172 us (11%)
  other arithmetic  44.5 us (3%)
  starting transfers between devices  29 us (2%)
  between operations  16.3 us (1%)
    dot_general x30, matrix products, product(): return jnp.einsum(formula, operand_a, operand_b, precision=HIGH)  618 us
    psum x1, waiting for transfers between devices, per_device(): summed = lax.psum((continued[0], continued[1]), 'depth')  563 us
    gather x2, local copies, waits for them, and re-layouts, per_device(): neighbours = padded[:, row_ids[:, :, None], col_ids[:, None, :]]  59.2 us
    all_to_all x1, waiting for transfers between devices, per_device(): lax.all_to_all(row_spectra[0], 'wide', split_axis=1, concat_axis=0, tiled...  57.7 us
    all_to_all x1, waiting for transfers between devices, per_device(): lax.all_to_all(row_spectra[1], 'wide', split_axis=1, concat_axis=0, tiled...  44.9 us
  transfers between devices with their start and end apart: 8, of which 5 were waited for; matrix products, arithmetic and copies ran while one was open for 14% of the time, Pallas kernels for 0%

commit v1 on v0

--- a/solution.py
+++ b/solution.py
@@ -1,3 +1,4 @@
+import functools
 import math
 import jax
 import jax.numpy as jnp
@@ -7,6 +8,16 @@
 RADIX = 128
 QLEV = 16
 HIGH = lax.Precision.HIGHEST
+
+
+def finish_forms(xin, axis_no, pos_dim):
+    odd = lax.axis_size("wide")
+    r_now = jnp.stack(jnp.split(xin, odd, axis_no))
+    next_value = lax.all_to_all(r_now, "wide", 0, 0)
+    return jnp.concatenate(next_value, pos_dim)
+
+
+convert_leaf_by_axis = functools.partial(finish_forms, axis_no=1, pos_dim=0)
 
 
 def padded_2(block, sides, width):
@@ -168,7 +179,7 @@
     )
     spectrum = column_forward(
         (
-            lax.all_to_all(row_spectra[0], "wide", split_axis=1, concat_axis=0, tiled=True),
+            convert_leaf_by_axis(row_spectra[0]),
             lax.all_to_all(row_spectra[1], "wide", split_axis=1, concat_axis=0, tiled=True),
         )
     )

time: 1580 us -> 1590 us (level)
  local copies, waits for them, and re-layouts: 172 us -> 196 us
  waiting for transfers between devices: 694 us -> 673 us
    unnamed x43 -> x66, local copies, waits for them, and re-layouts: 26.3 us -> 55.5 us
    all_to_all x1, waiting for transfers between devices: 44.9 us -> 24.1 us  [per_device(): lax.all_to_all(row_spectra[1], 'wide', split_axis=1, concat_axis=0, tiled...]
  transfers between devices with their start and end apart: 8 -> 8, of which waited for: 5 -> 5; matrix products, arithmetic and copies ran while one was open for 14% -> 16% of each run, Pallas kernels for 0% -> 0%
where the time goes in v1:
time: 1590 us; the launch traced here: 1580 us
  waiting for transfers between devices  673 us (42%)
  matrix products  616 us (39%)
  local copies, waits for them, and re-layouts  196 us (12%)
  other arithmetic  44.5 us (3%)
  starting transfers between devices  29.2 us (2%)
  between operations  16.3 us (1%)
    dot_general x30, matrix products, product(): return jnp.einsum(formula, operand_a, operand_b, precision=HIGH)  615 us
    psum x1, waiting for transfers between devices, per_device(): summed = lax.psum((continued[0], continued[1]), 'depth')  563 us
    gather x2, local copies, waits for them, and re-layouts, per_device(): neighbours = padded[:, row_ids[:, :, None], col_ids[:, None, :]]  59.8 us
    all_to_all x1, waiting for transfers between devices, finish_forms(): next_value = lax.all_to_all(r_now, 'wide', 0, 0)  57.7 us
    unnamed x66, local copies, waits for them, and re-layouts  55.5 us
  transfers between devices with their start and end apart: 8, of which 5 were waited for; matrix products, arithmetic and copies ran while one was open for 16% of the time, Pallas kernels for 0%

profile of v1, /device:TPU:0, one launch (start us, length us, event | category | flops | bytes accessed | tf_op | source)
XLA Modules:
  0.0 1575.2 jit_solution(10975354988440490705)
XLA Ops:
  79.8 18.5 %fusion.46 = f32[512,32,128]{0,2,1:T(8,128)S(1)} fusion(f32[512,32,128]{2,1,0:T(8,128)} %copy-done.5), kind=kOutput, calls=%fused_computation.69 | convolution fusion | flops 3221471232 | bytes 16777216 | tf_op jit(solution)/shard_map/rab,bc->rac/dot_general | solution.py:38
  98.3 19.2 %fusion.68 = f32[512,32,128]{0,2,1:T(8,128)S(1)} fusion(f32[512,32,128]{0,2,1:T(8,128)S(1)} %fusion.46, f32[512,32,128]{2,1,0:T(8,128)} %copy-done.2), kind=kOutput, calls=%fused_computation.97 | convolution fusion | flops 3223552000 | bytes 25165824 | tf_op jit(solution)/shard_map/rab,bc->rac/dot_general | solution.py:38
  150.4 24.1 %all-to-all-done.1 = f32[512,8,512]{2,0,1:T(8,128)} async-done(((f32[512,8,512]{2,0,1:T(8,128)}), f32[512,8,512]{2,0,1:T(8,128)}, u32[]{:S(2)}, u32[]{:S(2)}) %all-to-all-start.1) | async-done | bytes 8388640 | tf_op jit(solution)/shard_map/all_to_all | solution.py:183
  181.2 17.1 %fusion.36 = f32[32,128,512]{2,0,1:T(8,128)} fusion(f32[32,128,512]{2,1,0:T(8,128)} %bitcast.28), kind=kOutput, calls=%fused_computation.59 | convolution fusion | flops 805320704 | bytes 16777216 | tf_op jit(solution)/shard_map/bcd,ab->acd/dot_general | solution.py:38
  198.4 17.6 %fusion.38 = f32[32,128,512]{2,0,1:T(8,128)} fusion(f32[32,128,512]{2,1,0:T(8,128)} %bitcast.28), kind=kOutput, calls=%fused_computation.61 | convolution fusion | flops 805321728 | bytes 16777216 | tf_op jit(solution)/shard_map/bcd,ab->acd/dot_general | solution.py:38
  216.0 57.7 %all-to-all-done = f32[8,512,1,512]{3,1,2,0:T(8,128)} async-done(((f32[8,512,1,512]{3,1,2,0:T(8,128)}), f32[8,512,1,512]{3,1,2,0:T(8,128)}, u32[]{:S(2)}, u32[]{:S(2)}) %all-to-all-start) | async-done | bytes 8388640 | tf_op jit(solution)/shard_map/all_to_all | solution.py:16
  273.7 17.7 %fusion.42 = f32[32,128,512]{2,0,1:T(8,128)} fusion(f32[32,128,512]{2,1,0:T(8,128)} %bitcast.22), kind=kOutput, calls=%fused_computation.65 | convolution fusion | flops 805320704 | bytes 16777216 | tf_op jit(solution)/shard_map/bcd,ab->acd/dot_general | solution.py:38
  291.4 24.4 %multiply_subtract_fusion = (f32[32,128,512]{2,0,1:T(8,128)}, f32[32,128,512]{2,0,1:T(8,128)}) fusion(f32[32,128]{0,1:T(8,128)S(1)} %copy.163, f32[32,128]{0,1:T(8,128)S(1)} %copy.160, f32[32,128,512]{2,0,1:T(8,128)} %fusion.36, f32[32,128,512]{2,0,1:T(8,128)} %fusion.42, f32[32,128,512]{2,0,1:T(8,128)} %fusion.38, f32[32,128,512]{2,1,0:T(8,128)} %bitcast.22), kind=kOutput, calls=%fused_computation.48 | convolution fusion | flops 822098944 | bytes 50364416 | tf_op jit(solution)/shard_map/bcd,ab->acd/dot_general | solution.py:38
  315.8 18.1 %fusion.28 = f32[128,32,512]{2,0,1:T(8,128)S(1)} fusion(f32[32,128,512]{2,0,1:T(8,128)} %get-tuple-element.15), kind=kOutput, calls=%fused_computation.51 | convolution fusion | flops 3221454848 | bytes 16777216 | tf_op jit(solution)/shard_map/abd,bc->acd/dot_general | solution.py:38
  346.3 18.2 %bitcast_multiply_fusion.5 = f32[32,128,512]{2,1,0:T(8,128)} fusion(f32[128,32,512]{2,0,1:T(8,128)S(1)} %fusion.30, f32[]{:T(128)} %bitcast.220, f32[]{:T(128)} %bitcast.222, f32[32,128]{1,0:T(8,128)S(1)} %get-tuple-element.48, f32[512]{0:T(512)S(1)} %fusion.224, f32[32,128,512]{2,0,1:T(8,128)S(1)} %bitcast.232), kind=kOutput, calls=%fused_computation.40 | convolution fusion | flops 3240329216 | bytes 25184264 | tf_op jit(solution)/shard_map/abd,bc->acd/dot_general | solution.py:38
  364.5 18.5 %bitcast_multiply_fusion.4 = f32[32,128,512]{2,1,0:T(8,128)} fusion(f32[128,32,512]{2,0,1:T(8,128)S(1)} %fusion.28, f32[]{:T(128)} %bitcast.221, f32[]{:T(128)} %bitcast.223, f32[32,128]{1,0:T(8,128)S(1)} %get-tuple-element.48, f32[512]{0:T(512)S(1)} %fusion.224, f32[32,128,512]{2,0,1:T(8,128)S(1)} %bitcast.232), kind=kOutput, calls=%fused_computation.39 | convolution fusion | flops 3240345600 | bytes 25184264 | tf_op jit(solution)/shard_map/abd,bc->acd/dot_general | solution.py:38
  383.3 563.2 %all-reduce.3.cloned.1.call-done = (f32[32,128,512]{2,1,0:T(8,128)}, f32[32,128,512]{2,1,0:T(8,128)}) async-done(((f32[32,128,512]{2,1,0:T(8,128)}, f32[32,128,512]{2,1,0:T(8,128)}), (f32[32,128,512]{2,1,0:T(8,128)}, f32[32,128,512]{2,1,0:T(8,128)})) %all-reduce.3.cloned.1.call-update) | async-done | bytes 16777232 | tf_op jit(solution)/shard_map/psum | solution.py:210
  946.5 21.0 %add_bitcast_fusion.1 = (f32[1,32,128,512]{3,2,1,0:T(8,128)}, f32[1,32,128,512]{3,2,1,0:T(8,128)S(1)}, f32[1,32,128,512]{3,2,1,0:T(8,128)}, f32[1,32,128,512]{3,...) fusion(f32[32,128,512]{2,1,0:T(8,128)} %get-tuple-element.10, ...), kind=kLoop, calls=%fused_computation.43 | loop fusion | flops 54525952 | bytes 67166208 | tf_op jit(solution)/shard_map/stack | solution.py:133
  967.5 34.1 %fusion.10 = f32[128,3,32,512]{3,0,2,1:T(8,128)} fusion(f32[1,32,128,512]{3,2,1,0:T(8,128)} %get-tuple-element.28, f32[1,32,128,512]{3,2,1,0:T(8,128)} %get-tuple-element.31, f32[1,32,128,512]{3,2,1,0:T(8,128)} %get-tuple-element.18), kind=kOutput, calls=%fused_computation.18 | convolution fusion | flops 9676488704 | bytes 50331648 | tf_op jit(solution)/shard_map/jabd,cb->jacd/dot_general | solution.py:38
  1001.6 29.1 %fusion.11 = f32[128,3,32,512]{3,0,2,1:T(8,128)} fusion(f32[1,32,128,512]{3,2,1,0:T(8,128)} %get-tuple-element.28, f32[1,32,128,512]{3,2,1,0:T(8,128)} %get-tuple-element.31, f32[1,32,128,512]{3,2,1,0:T(8,128)} %get-tuple-element.18), kind=kOutput, calls=%fused_computation.19 | convolution fusion | flops 9676488704 | bytes 50331648 | tf_op jit(solution)/shard_map/jabd,cb->jacd/dot_general | solution.py:38
  1030.8 28.4 %fusion.13 = f32[128,3,32,512]{3,0,2,1:T(8,128)} fusion(f32[1,32,128,512]{3,2,1,0:T(8,128)S(1)} %get-tuple-element.29, f32[1,32,128,512]{3,2,1,0:T(8,128)} %get-tuple-element.30, f32[1,32,128,512]{3,2,1,0:T(8,128)S(1)} %get-tuple-element.19), kind=kOutput, calls=%fused_computation.21 | convolution fusion | flops 9676488704 | bytes 50331648 | tf_op jit(solution)/shard_map/jabd,cb->jacd/dot_general | solution.py:38
  1059.2 60.9 %fusion = (f32[3,32,128,512]{3,2,1,0:T(8,128)}, f32[3,32,128,512]{3,2,1,0:T(8,128)}) fusion(f32[32,128]{1,0:T(8,128)S(1)} %fusion.189, f32[32,128]{1,0:T(8,128)S(1)} %get-tuple-element.51, f32[128,3,32,512]{3,0,2,1:T(8,128)} %fusion.10, f32[128,3,32,512]{3,0,2,1:T(8,128)} %fusion.13, f32[128,3,32,512]{3,0,2,1:T(8,128)} %fusion.11, ...), kind=kOutput, calls=%fused_computation.5 | convolution fusion | flops 9726820352 | bytes 151027712 | tf_op jit(solution)/shard_map/jabd,cb->jacd/dot_general | solution.py:38
  1120.1 34.6 %fusion.2 = f32[8,3,128,512]{3,0,2,1:T(8,128)} fusion(f32[3,32,128,512]{3,2,1,0:T(8,128)} %get-tuple-element.13, f32[32,32]{1,0:T(8,128)S(1)} %fusion.192, s32[]{:T(128)S(6)} %select_n.307), kind=kOutput, calls=%fused_computation.10 | convolution fusion | flops 603979776 | bytes 31461380 | tf_op jit(solution)/shard_map/jbcd,ab->jacd/dot_general | solution.py:38
  1154.7 26.1 %add_bitcast_fusion.4 = f32[3,8,128,512]{3,1,2,0:T(8,128)S(1)} fusion(f32[8,3,128,512]{3,0,2,1:T(8,128)} %fusion.2, f32[3,32,128,512]{3,2,1,0:T(8,128)S(1)} %copy-done, f32[32,32]{1,0:T(8,128)S(1)} %fusion.191, s32[]{:T(128)S(6)} %select_n.307), kind=kOutput, calls=%fused_computation.79 | convolution fusion | flops 605552640 | bytes 37752836 | tf_op jit(solution)/shard_map/jbcd,ab->jacd/dot_general | solution.py:38
  1191.9 33.3 %fusion.4 = f32[8,3,128,512]{3,0,2,1:T(8,128)S(1)} fusion(f32[3,32,128,512]{3,2,1,0:T(8,128)} %get-tuple-element.13, f32[32,32]{1,0:T(8,128)S(1)} %fusion.191, s32[]{:T(128)S(6)} %select_n.307), kind=kOutput, calls=%fused_computation.12 | convolution fusion | flops 603979776 | bytes 31461380 | tf_op jit(solution)/shard_map/jbcd,ab->jacd/dot_general | solution.py:38
  1225.2 33.7 %subtract_bitcast_fusion.6 = f32[3,8,128,512]{3,1,2,0:T(8,128)S(1)} fusion(f32[8,3,128,512]{3,0,2,1:T(8,128)S(1)} %fusion.4, f32[3,32,128,512]{3,2,1,0:T(8,128)} %get-tuple-element.12, f32[32,32]{1,0:T(8,128)S(1)} %fusion.192, s32[]{:T(128)S(6)} %select_n.307), kind=kOutput, calls=%fused_computation.80 | convolution fusion | flops 605552640 | bytes 37752836 | tf_op jit(solution)/shard_map/jbcd,ab->jacd/dot_general | solution.py:38
  1317.8 24.1 %all-to-all-done.2 = f32[3,8,128,512]{3,2,0,1:T(8,128)} async-done(((f32[3,8,128,512]{3,2,0,1:T(8,128)}), f32[3,8,128,512]{3,2,0,1:T(8,128)}, u32[]{:S(2)}, u32[]{:S(2)}) %all-to-all-start.2) | async-done | bytes 6291488 | tf_op jit(solution)/shard_map/all_to_all | solution.py:227
  1479.2 55.7 %gather_fusion = f32[4096,6]{0,1:T(8,128)S(1)} fusion(f32[6,132,4096]{2,0,1:T(8,128)} %pad_maximum_fusion.6, s32[4096]{0:T(1024)S(1)} %reshape.407), kind=kCustom, calls=%fused_computation | custom fusion | bytes 229376 | tf_op jit(solution)/shard_map/gather | solution.py:248
  1548.1 17.8 %copy.196 = f32[6,128,4096]{2,1,0:T(8,128)} copy(f32[6,128,4096]{2,0,1:T(8,128)} %copy-done.1) | data formatting | bytes 25165824
  (146 shorter events, 345.8 us)
Async XLA Ops:
  12.5 9.6 copy-start.6
  35.1 14.0 copy-start.5
  35.2 14.0 copy-start.2
  74.6 99.8 %all-to-all-start.1 = ((f32[512,8,512]{2,0,1:T(8,128)}), f32[512,8,512]{2,0,1:T(8,128)}, u32[]{:S(2)}, u32[]{:S(2)}) async-start(f32[512,8,512]{2,0,1:T(8,128)} %copy.158), calls=%async_computation.1 | async-start | bytes 16777216 | tf_op jit(solution)/shard_map/all_to_all | solution.py:183
  134.2 14.0 copy-start.12
  135.5 13.8 copy-start.11
  136.8 10.4 copy-start.13
  174.4 99.3 %all-to-all-start = ((f32[8,512,1,512]{3,1,2,0:T(8,128)}), f32[8,512,1,512]{3,1,2,0:T(8,128)}, u32[]{:S(2)}, u32[]{:S(2)}) async-start(f32[8,512,1,512]{3,1,2,0:T(8,128)} %bitcast_dynamic-update-slice_fusion), calls=%async_computation | async-start | bytes 16777216 | tf_op jit(solution)/shard_map/all_to_all | solution.py:16
  179.6 766.8 %all-reduce.3.cloned.1.call-start = ((), (), s32[]{:S(2)}) async-start(), calls=%async_computation.5 | async-start | bytes 33554432 | tf_op jit(solution)/shard_map/psum | solution.py:210
  315.8 18.1 %copy-start.7 = (f32[32,128,512]{2,0,1:T(8,128)S(1)}, f32[32,128,512]{2,0,1:T(8,128)}, u32[]{:S(2)}) copy-start(f32[32,128,512]{2,0,1:T(8,128)} %get-tuple-element.15) | copy-start | bytes 25165828
  315.8 30.5 %slice-start.2 = ((s8[8388608]{0:T(1024)(128)(4,1)}), s8[4194304]{0:T(1024)(128)(4,1)S(1)}, s32[]{:S(2)}) async-start(s8[8388608]{0:T(1024)(128)(4,1)} %bitcast.231), calls=%async_computation.8 | async-start | bytes 8388608
  333.9 12.4 slice-start.3
  967.5 63.3 %copy-start.3 = (f32[1,32,128,512]{3,2,1,0:T(8,128)}, f32[1,32,128,512]{3,2,1,0:T(8,128)S(1)}, u32[]{:S(2)}) copy-start(f32[1,32,128,512]{3,2,1,0:T(8,128)S(1)} %get-tuple-element.19) | copy-start | bytes 25165828
  967.5 63.3 %copy-start.4 = (f32[1,32,128,512]{3,2,1,0:T(8,128)}, f32[1,32,128,512]{3,2,1,0:T(8,128)S(1)}, u32[]{:S(2)}) copy-start(f32[1,32,128,512]{3,2,1,0:T(8,128)S(1)} %get-tuple-element.29) | copy-start | bytes 25165828
  1120.1 34.6 %copy-start = (f32[3,32,128,512]{3,2,1,0:T(8,128)S(1)}, f32[3,32,128,512]{3,2,1,0:T(8,128)}, u32[]{:S(2)}) copy-start(f32[3,32,128,512]{3,2,1,0:T(8,128)} %get-tuple-element.12) | copy-start | bytes 75497472
  1187.2 78.0 %all-to-all-start.3 = ((f32[3,8,128,512]{3,2,0,1:T(8,128)}), f32[3,8,128,512]{3,2,0,1:T(8,128)}, u32[]{:S(2)}, u32[]{:S(2)}) async-start(f32[3,8,128,512]{3,2,0,1:T(8,128)} %copy.179), calls=%async_computation.3 | async-start | bytes 12582912 | tf_op jit(solution)/shard_map/all_to_all | solution.py:228
  1265.2 76.7 %all-to-all-start.2 = ((f32[3,8,128,512]{3,2,0,1:T(8,128)}), f32[3,8,128,512]{3,2,0,1:T(8,128)}, u32[]{:S(2)}, u32[]{:S(2)}) async-start(f32[3,8,128,512]{3,2,0,1:T(8,128)} %copy.174), calls=%async_computation.2 | async-start | bytes 12582912 | tf_op jit(solution)/shard_map/all_to_all | solution.py:227
  1291.7 13.7 copy-start.8
  1357.8 13.9 copy-start.9
  1387.3 19.0 %slice-start = ((s8[6291456]{0:T(1024)(128)(4,1)}), s8[4194304]{0:T(1024)(128)(4,1)S(1)}, s32[]{:S(2)}) async-start(s8[6291456]{0:T(1024)(128)(4,1)} %bitcast.226), calls=%async_computation.6 | async-start | bytes 8388608
  1396.6 9.7 slice-start.1
  1463.1 9.5 collective-permute-start
  1463.2 9.5 collective-permute-start.1
  1544.5 21.4 %all-to-all-start.4 = ((f32[8,1,384]{2,1,0:T(1,128)}), f32[8,1,384]{2,1,0:T(1,128)S(1)}, u32[]{:S(2)}, u32[]{:S(2)}) async-start(f32[8,1,384]{2,1,0:T(1,128)} %reshape.434), calls=%async_computation.4 | async-start | bytes 24576 | tf_op jit(solution)/shard_map/all_to_all | solution.py:264
  (7 other events, 47.9 us)
Sparse Core Ops, SparseCore 0:
  383.1 563.3 all-reduce.2
